TPU v7x, 32 devices: a whole 2x2x4 slice. The times are simulated.
32 devices in a mesh: freq: 2 (over y), row: 4 (over z), col: 4 (over x, core).
Axes of the slice: x: 2, y: 2, z: 4, core: 2. Of those that a mesh axis runs over, the one named last changes fastest.
Arguments:
- traces: bfloat16 [4, 6144, 6144], P('freq', 'row', 'col'), parts along dimension 0, may hold values from -6 to 6
- recv_live: int32 [12288], P('freq'), parts along dimension 0, may hold values 0 or 1
- missing: int32 [8, 96], P('freq'), parts along dimension 0, may hold values from 0 to 1535, as said below
- wavelet: float32 [4], P('freq'), parts along dimension 0, may hold values from 0.5 to 1.5
Outputs:
- primaries: float32 [4, 6144, 512], P('freq', 'row', 'col'), parts along dimension 0
There are 2 independent parts, one for each index of `freq`. A program takes and returns all parts, laid end to end along the dimension named above; each array names one. Nothing has to cross between parts.
Inputs may be any that keep to these rules, and one draw needn't show every extreme that they name: `missing`: each row lists 96 distinct positions within one block of 1536 shots, the shots of that block that were not recorded; the block's first and last shots are always among them.
All inputs are finite; a program needn't handle non-finite values.
Results may differ from a plain program's by a relative error of at most 0.0003.
Values may be sent and summed in bfloat16 or wider, within the bound.
A program may use at most 128 MiB of HBM per device.

v0:
```python
import math

import jax
import jax.numpy as jnp
from jax import lax
from jax.sharding import PartitionSpec as P

ORDER = 6144
WIN = 128


def from_behind(block, axis, distance):
    devices = range(lax.axis_size(axis))
    route = [((i - distance) % len(devices), i) for i in devices]
    return lax.ppermute(block, axis, route)


def matmul(first, second):
    return jnp.dot(first, second, preferred_element_type=jnp.float32)


def complex_product(left_tile, right_tile):
    real_part = matmul(left_tile[0], right_tile[0]) - matmul(left_tile[1], right_tile[1])
    imag_part = matmul(left_tile[0], right_tile[1]) + matmul(left_tile[1], right_tile[0])
    return jnp.stack([real_part, imag_part])


def mirror(payload, grid_size, row_index, col_index):
    anti_sum = row_index + col_index
    anchors = jnp.arange(grid_size, dtype=jnp.int32)
    bit_count = grid_size.bit_length() - 1
    for bit_number in range(bit_count):
        stride = 2**bit_number
        carried = from_behind(payload, "row", stride)
        carried = from_behind(carried, "col", grid_size - stride)
        offset = (anti_sum - 2 * anchors) % grid_size
        spot_row = (anchors + offset % stride) % grid_size
        arrive = jnp.any(
            (spot_row == (row_index - stride) % grid_size) & (offset // stride % 2 == 1)
        )
        payload = jnp.where(arrive, carried, payload)
    return payload


def transpose_blocks(payload, grid_size, row_index, col_index):
    anti_sum = row_index + col_index
    anchors = jnp.arange(grid_size, dtype=jnp.int32)
    bit_count = grid_size.bit_length() - 1
    for bit_number in range(bit_count):
        stride = 2**bit_number
        carried = from_behind(payload, "row", stride)
        carried = from_behind(carried, "col", grid_size - stride)
        offset = (anti_sum - 2 * anchors) % grid_size
        spot_row = (anchors + offset % stride) % grid_size
        arrive = jnp.any(
            (spot_row == (row_index - stride) % grid_size) & (offset // stride % 2 == 1)
        )
        payload = jnp.where(arrive, carried, payload)
    return payload


def local(traces, recv_live, missing, wavelet):
    tile_size = traces.shape[1]
    grid_size = lax.axis_size("row")
    row_index = lax.axis_index("row")
    col_index = lax.axis_index("col")
    positions = jnp.arange(tile_size, dtype=jnp.int32)
    miss_row = lax.dynamic_index_in_dim(missing, row_index, 0, keepdims=False)
    miss_col = lax.dynamic_index_in_dim(missing, col_index, 0, keepdims=False)
    dead_row = jnp.any(positions[:, None] == miss_row[None, :], axis=1)
    dead_col = jnp.any(positions[:, None] == miss_col[None, :], axis=1)
    recv_row = lax.dynamic_slice_in_dim(recv_live, row_index * tile_size, tile_size) == 1
    recv_col = lax.dynamic_slice_in_dim(recv_live, col_index * tile_size, tile_size) == 1
    zero_bf = jnp.zeros((), jnp.bfloat16)
    outgoing = jnp.swapaxes(jnp.take(traces, miss_col, axis=2), 1, 2)
    incoming = mirror(outgoing, grid_size, row_index, col_index)
    direct = jnp.where(recv_col[None, None, :], traces, zero_bf)
    direct = jnp.where(dead_row[None, :, None], zero_bf, direct)
    keep_mask = jnp.take(recv_row, miss_row)[:, None] & jnp.logical_not(dead_col)[None, :]
    patched = jnp.where(keep_mask[None], incoming, zero_bf)
    filled = direct.at[:, miss_row, :].set(patched)
    window = filled[:, :, :WIN]
    win_width = window.shape[2]
    running = jnp.zeros((2, tile_size, win_width), jnp.float32)
    swapped = transpose_blocks(window, grid_size, row_index, col_index)
    gathered = lax.all_gather(swapped, "row", axis=2, tiled=True)

    def one_hop(stop_index, total):
        source_block = (col_index - stop_index - 1) % grid_size
        piece = lax.dynamic_slice_in_dim(gathered, source_block * win_width, win_width, 2)
        total = total + complex_product(filled, piece)
        return from_behind(total, "col", 1)

    running = lax.fori_loop(0, grid_size - 1, one_hop, running)
    own_piece = lax.dynamic_slice_in_dim(gathered, col_index * win_width, win_width, 2)
    running = running + complex_product(filled, own_piece)
    norm_scale = 1.0 / math.sqrt(ORDER)
    pred_real = (wavelet[0] * running[0] - wavelet[1] * running[1]) * norm_scale
    pred_imag = (wavelet[0] * running[1] + wavelet[1] * running[0]) * norm_scale
    window_f = window.astype(jnp.float32)
    return jnp.stack([window_f[0] - pred_real, window_f[1] - pred_imag])


def solution(mesh):
    in_specs = (P("freq", "row", "col"), P("freq"), P("freq", None), P("freq"))
    out_specs = P("freq", "row", "col")
    return jax.shard_map(local, mesh=mesh, in_specs=in_specs, out_specs=out_specs, check_vma=False)
```

profile of v0, /device:TPU:1, one launch (start us, length us, event | category | flops | bytes accessed | tf_op | source)
XLA Modules:
  0.0 445.7 jit_solution(11039672735321170451)
XLA Ops:
  10.2 24.0 %copy.16 = bf16[2,1536,1536]{1,0,2:T(2,128)(2,1)} copy(bf16[2,1536,1536]{2,1,0:T(8,128)(2,1)} %param.6) | data formatting | bytes 18874368 | tf_op args[0]
  34.2 5.5 %gather_fusion.1 = bf16[96,2,1536]{2,1,0:T(2,128)(2,1)S(1)} fusion(bf16[2,1536,1536]{1,0,2:T(2,128)(2,1)} %copy.16, s32[1024]{0:T(1024)S(1)} %get-tuple-element.183), kind=kCustom, calls=%fused_computation.1 | custom fusion | bytes 1180032 | tf_op jit(solution)/shard_map/jit(_take)/gather | solution.py:75
  42.5 15.0 %collective-permute-done.1 = bf16[2,96,1536]{2,0,1:T(2,128)(2,1)S(1)} collective-permute-done((bf16[2,96,1536]{2,0,1:T(2,128)(2,1)S(1)}, bf16[2,96,1536]{2,0,1:T(2,128)(2,1)S(1)}, u32[]{:S(2)}, u32[]{:S(2)}) %collective-permute-start.1) | collective-permute-done | bytes 589856 | tf_op jit(solution)/shard_map/ppermute | solution.py:15
  59.4 8.0 %collective-permute-done.2 = bf16[2,96,1536]{2,0,1:T(2,128)(2,1)S(1)} collective-permute-done((bf16[2,96,1536]{2,0,1:T(2,128)(2,1)S(1)}, bf16[2,96,1536]{2,0,1:T(2,128)(2,1)S(1)}, u32[]{:S(2)}, u32[]{:S(2)}) %collective-permute-start.2) | collective-permute-done | bytes 589856 | tf_op jit(solution)/shard_map/ppermute | solution.py:15
  69.6 26.6 %collective-permute-done.3 = bf16[2,96,1536]{2,0,1:T(2,128)(2,1)S(1)} collective-permute-done((bf16[2,96,1536]{2,0,1:T(2,128)(2,1)S(1)}, bf16[2,96,1536]{2,0,1:T(2,128)(2,1)S(1)}, u32[]{:S(2)}, u32[]{:S(2)}) %collective-permute-start.3) | collective-permute-done | bytes 589856 | tf_op jit(solution)/shard_map/ppermute | solution.py:15
  97.3 42.0 %broadcast_select_fusion = bf16[2,1536,1536]{2,0,1:T(2,128)(2,1)} fusion(pred[1536]{0:T(1024)(128)(4,1)S(1)} %fusion.54, pred[1536]{0:T(1024)(128)(4,1)S(1)} %get-tuple-element.175, bf16[2,1536,1536]{2,1,0:T(8,128)(2,1)} %param.6), kind=kLoop, calls=%fused_computation.26 | loop fusion | flops 9437184 | bytes 18877440 | tf_op jit(solution)/shard_map/jit(_where)/select_n | solution.py:78
  141.9 11.6 %scatter_fusion = bf16[2,1536,1536]{2,0,1:T(2,128)(2,1)} fusion(bf16[2,1536,1536]{2,0,1:T(2,128)(2,1)} %broadcast_select_fusion, s32[96]{0:T(128)S(1)} %get-tuple-element.178, bf16[96,2,1536]{2,1,0:T(2,128)(2,1)S(1)} %fusion.52), kind=kCustom, calls=%fused_computation.2 | custom fusion | bytes 1769856 | tf_op jit(solution)/shard_map/scatter | solution.py:81
  153.6 8.8 %copy.17 = bf16[2,1536,1536]{2,1,0:T(8,128)(2,1)} copy(bf16[2,1536,1536]{2,0,1:T(2,128)(2,1)} %scatter_fusion) | data formatting | bytes 18874368 | tf_op jit(solution)/shard_map/scatter | solution.py:81
  163.7 20.2 %collective-permute-done.5 = bf16[2,1536,128]{2,1,0:T(8,128)(2,1)S(1)} collective-permute-done((bf16[2,1536,128]{2,1,0:T(8,128)(2,1)S(1)}, bf16[2,1536,128]{2,1,0:T(8,128)(2,1)S(1)}, u32[]{:S(2)}, u32[]{:S(2)}) %collective-permute-start.5) | collective-permute-done | bytes 786464 | tf_op jit(solution)/shard_map/ppermute | solution.py:15
  185.4 9.9 %collective-permute-done.6 = bf16[2,1536,128]{2,1,0:T(8,128)(2,1)S(1)} collective-permute-done((bf16[2,1536,128]{2,1,0:T(8,128)(2,1)S(1)}, bf16[2,1536,128]{2,1,0:T(8,128)(2,1)S(1)}, u32[]{:S(2)}, u32[]{:S(2)}) %collective-permute-start.6) | collective-permute-done | bytes 786464 | tf_op jit(solution)/shard_map/ppermute | solution.py:15
  198.4 35.3 %collective-permute-done.7 = bf16[2,1536,128]{2,1,0:T(8,128)(2,1)S(1)} collective-permute-done((bf16[2,1536,128]{2,1,0:T(8,128)(2,1)S(1)}, bf16[2,1536,128]{2,1,0:T(8,128)(2,1)S(1)}, u32[]{:S(2)}, u32[]{:S(2)}) %collective-permute-start.7) | collective-permute-done | bytes 786464 | tf_op jit(solution)/shard_map/ppermute | solution.py:15
  234.2 18.2 %collective-permute-done.8 = bf16[2,1536,128]{2,1,0:T(8,128)(2,1)S(1)} collective-permute-done((bf16[2,1536,128]{2,1,0:T(8,128)(2,1)S(1)}, bf16[2,1536,128]{2,1,0:T(8,128)(2,1)S(1)}, u32[]{:S(2)}, u32[]{:S(2)}) %collective-permute-start.8) | collective-permute-done | bytes 786464 | tf_op jit(solution)/shard_map/ppermute | solution.py:15
  254.6 19.5 %fusion.69 = (bf16[1,1536,1536]{2,0,1:T(2,128)(2,1)}, bf16[1,1536,1536]{2,0,1:T(2,128)(2,1)}) fusion(bf16[2,1536,1536]{2,0,1:T(2,128)(2,1)} %scatter_fusion), kind=kLoop, calls=%fused_computation.104 | loop fusion | bytes 18874368 | tf_op jit(solution)/shard_map/slice | solution.py:23
  274.1 41.9 %all-gather.2.cloned.1.call-done = bf16[2,1536,512]{2,1,0:T(8,128)(2,1)} async-done(((bf16[2,1536,128]{2,1,0:T(8,128)(2,1)}), bf16[2,1536,512]{2,1,0:T(8,128)(2,1)}) %all-gather.2.cloned.1.call-update) | async-done | bytes 3145744 | tf_op jit(solution)/shard_map/all_gather | solution.py:86
  316.2 102.6 %while.15 = (s32[]{:T(128)}, f32[2,1536,128]{1,2,0:T(8,128)S(1)}, s32[]{:T(128)}, bf16[2,1536,512]{2,1,0:T(8,128)(2,1)}, bf16[2,1536,1536]{2,1,0:T(8,128)(2,1)},...) while((s32[]{:T(128)}, f32[2,1536,128]{1,2,0:T(8,128)S(1)}, ...), condition=%wide.region_6.7_spmd, body=%wide.region_5.6_spmd.sunk | while | flops 2417098752 | bytes 73925016 | solution.py:94
  316.2 4.3 fusion.83
  320.5 4.2 fusion.85
  333.6 17.4 %collective-permute-done = f32[2,1536,128]{1,2,0:T(8,128)S(1)} collective-permute-done((f32[2,1536,128]{1,2,0:T(8,128)S(1)}, f32[2,1536,128]{1,2,0:T(8,128)S(1)}, u32[]{:S(2)}, u32[]{:S(2)}) %collective-permute-start) | collective-permute-done | bytes 1572896 | tf_op jit(solution)/shard_map/while/body/eval_jaxpr/ppermute | solution.py:15
  350.9 4.3 fusion.83
  367.5 17.4 %collective-permute-done = f32[2,1536,128]{1,2,0:T(8,128)S(1)} collective-permute-done((f32[2,1536,128]{1,2,0:T(8,128)S(1)}, f32[2,1536,128]{1,2,0:T(8,128)S(1)}, u32[]{:S(2)}, u32[]{:S(2)}) %collective-permute-start) | collective-permute-done | bytes 1572896 | tf_op jit(solution)/shard_map/while/body/eval_jaxpr/ppermute | solution.py:15
  384.9 4.3 fusion.83
  401.4 17.4 %collective-permute-done = f32[2,1536,128]{1,2,0:T(8,128)S(1)} collective-permute-done((f32[2,1536,128]{1,2,0:T(8,128)S(1)}, f32[2,1536,128]{1,2,0:T(8,128)S(1)}, u32[]{:S(2)}, u32[]{:S(2)}) %collective-permute-start) | collective-permute-done | bytes 1572896 | tf_op jit(solution)/shard_map/while/body/eval_jaxpr/ppermute | solution.py:15
  419.3 5.2 %fusion.28 = f32[1536,128]{1,0:T(8,128)S(1)} fusion(bf16[1,1536,1536]{2,0,1:T(2,128)(2,1)} %get-tuple-element.170, bf16[2,1536,512]{2,1,0:T(8,128)(2,1)} %get-tuple-element.269, s32[]{:T(128)S(6)} %select_n.231), kind=kOutput, calls=%fused_computation.28 | convolution fusion | flops 603979776 | bytes 10616836 | tf_op jit(solution)/shard_map/dot_general | solution.py:19
  424.5 5.3 %fusion.30 = f32[1536,128]{1,0:T(8,128)S(1)} fusion(bf16[1,1536,1536]{2,0,1:T(2,128)(2,1)} %get-tuple-element.170, bf16[2,1536,512]{2,1,0:T(8,128)(2,1)} %get-tuple-element.269, s32[]{:T(128)S(6)} %add.229, s32[]{:T(128)S(6)} %select_n.231), kind=kOutput, calls=%fused_computation.30 | convolution fusion | flops 603979776 | bytes 10616840 | tf_op jit(solution)/shard_map/dot_general | solution.py:19
  (67 shorter events, 65.8 us)
Async XLA Ops:
  6.5 309.5 %all-gather.2.cloned.1.call-start = ((), (), s32[]{:S(2)}) async-start(), calls=%async_computation | async-start | bytes 3932160 | tf_op jit(solution)/shard_map/all_gather | solution.py:86
  40.3 17.2 %collective-permute-start.1 = (bf16[2,96,1536]{2,0,1:T(2,128)(2,1)S(1)}, bf16[2,96,1536]{2,0,1:T(2,128)(2,1)S(1)}, u32[]{:S(2)}, u32[]{:S(2)}) collective-permute-start(bf16[2,96,1536]{2,0,1:T(2,128)(2,1)S(1)} %fusion.53), channel_id=1, source_target_pairs={{12,0},{0,4},{4,8},{8,12},{13,1},{1,5},{5,9},{9,13},{14,2},{2,6},{... | collective-permute-start | bytes 1769480 | tf_op jit(solution)/shard_map/ppermute | solution.py:15
  57.5 10.0 %collective-permute-start.2 = (bf16[2,96,1536]{2,0,1:T(2,128)(2,1)S(1)}, bf16[2,96,1536]{2,0,1:T(2,128)(2,1)S(1)}, u32[]{:S(2)}, u32[]{:S(2)}) collective-permute-start(bf16[2,96,1536]{2,0,1:T(2,128)(2,1)S(1)} %collective-permute-done.1), channel_id=1, source_target_pairs={{1,0},{2,1},{3,2},{0,3},{5,4},{6,5},{7,6},{4,7},{9,8},{10,9},{11,1... | collective-permute-start | bytes 1769480 | tf_op jit(solution)/shard_map/ppermute | solution.py:15
  68.9 27.3 %collective-permute-start.3 = (bf16[2,96,1536]{2,0,1:T(2,128)(2,1)S(1)}, bf16[2,96,1536]{2,0,1:T(2,128)(2,1)S(1)}, u32[]{:S(2)}, u32[]{:S(2)}) collective-permute-start(bf16[2,96,1536]{2,0,1:T(2,128)(2,1)S(1)} %broadcast_select_fusion.3), channel_id=1, source_target_pairs={{8,0},{12,4},{0,8},{4,12},{9,1},{13,5},{1,9},{5,13},{10,2},{14,6},... | collective-permute-start | bytes 1769480 | tf_op jit(solution)/shard_map/ppermute | solution.py:15
  96.2 44.0 %collective-permute-start.4 = (bf16[2,96,1536]{2,0,1:T(2,128)(2,1)S(1)}, bf16[2,96,1536]{2,0,1:T(2,128)(2,1)S(1)}, u32[]{:S(2)}, u32[]{:S(2)}) collective-permute-start(bf16[2,96,1536]{2,0,1:T(2,128)(2,1)S(1)} %collective-permute-done.3), channel_id=1, source_target_pairs={{2,0},{3,1},{0,2},{1,3},{6,4},{7,5},{4,6},{5,7},{10,8},{11,9},{8,1... | collective-permute-start | bytes 1769480 | tf_op jit(solution)/shard_map/ppermute | solution.py:15
  162.4 91.6 %copy-start.2 = (f32[2]{0:T(128)S(1)}, f32[2]{0:T(128)}, u32[]{:S(2)}) copy-start(f32[2]{0:T(128)} %param.9) | copy-start | bytes 28
  163.6 20.3 %collective-permute-start.5 = (bf16[2,1536,128]{2,1,0:T(8,128)(2,1)S(1)}, bf16[2,1536,128]{2,1,0:T(8,128)(2,1)S(1)}, u32[]{:S(2)}, u32[]{:S(2)}) collective-permute-start(bf16[2,1536,128]{2,1,0:T(8,128)(2,1)S(1)} %slice.100), channel_id=1, source_target_pairs={{12,0},{0,4},{4,8},{8,12},{13,1},{1,5},{5,9},{9,13},{14,2},{2,6},{... | collective-permute-start | bytes 2359304 | tf_op jit(solution)/shard_map/ppermute | solution.py:15
  183.9 11.4 %collective-permute-start.6 = (bf16[2,1536,128]{2,1,0:T(8,128)(2,1)S(1)}, bf16[2,1536,128]{2,1,0:T(8,128)(2,1)S(1)}, u32[]{:S(2)}, u32[]{:S(2)}) collective-permute-start(bf16[2,1536,128]{2,1,0:T(8,128)(2,1)S(1)} %collective-permute-done.5), channel_id=1, source_target_pairs={{1,0},{2,1},{3,2},{0,3},{5,4},{6,5},{7,6},{4,7},{9,8},{10,9},{11,1... | collective-permute-start | bytes 2359304 | tf_op jit(solution)/shard_map/ppermute | solution.py:15
  198.4 35.3 %collective-permute-start.7 = (bf16[2,1536,128]{2,1,0:T(8,128)(2,1)S(1)}, bf16[2,1536,128]{2,1,0:T(8,128)(2,1)S(1)}, u32[]{:S(2)}, u32[]{:S(2)}) collective-permute-start(bf16[2,1536,128]{2,1,0:T(8,128)(2,1)S(1)} %get-tuple-element.171), channel_id=1, source_target_pairs={{8,0},{12,4},{0,8},{4,12},{9,1},{13,5},{1,9},{5,13},{10,2},{14,6},... | collective-permute-start | bytes 2359304 | tf_op jit(solution)/shard_map/ppermute | solution.py:15
  233.7 18.7 %collective-permute-start.8 = (bf16[2,1536,128]{2,1,0:T(8,128)(2,1)S(1)}, bf16[2,1536,128]{2,1,0:T(8,128)(2,1)S(1)}, u32[]{:S(2)}, u32[]{:S(2)}) collective-permute-start(bf16[2,1536,128]{2,1,0:T(8,128)(2,1)S(1)} %collective-permute-done.7), channel_id=1, source_target_pairs={{2,0},{3,1},{0,2},{1,3},{6,4},{7,5},{4,6},{5,7},{10,8},{11,9},{8,1... | collective-permute-start | bytes 2359304 | tf_op jit(solution)/shard_map/ppermute | solution.py:15
  316.2 8.5 %copy-start = (bf16[2,1536,1536]{2,1,0:T(8,128)(2,1)S(1)}, bf16[2,1536,1536]{2,1,0:T(8,128)(2,1)}, u32[]{:S(2)}) copy-start(bf16[2,1536,1536]{2,1,0:T(8,128)(2,1)} %get-tuple-element.246) | copy-start | bytes 28311556 | tf_op jit(solution)/shard_map/while
  330.3 20.7 %collective-permute-start = (f32[2,1536,128]{1,2,0:T(8,128)S(1)}, f32[2,1536,128]{1,2,0:T(8,128)S(1)}, u32[]{:S(2)}, u32[]{:S(2)}) collective-permute-start(f32[2,1536,128]{1,2,0:T(8,128)S(1)} %maximum_add_fusion.3), channel_id=1, source_target_pairs={{3,0},{0,1},{1,2},{2,3},{7,4},{4,5},{5,6},{6,7},{11,8},{8,9},{9,10... | collective-permute-start | bytes 4718600 | tf_op jit(solution)/shard_map/while/body/eval_jaxpr/ppermute | solution.py:15
  350.9 8.5 %copy-start = (bf16[2,1536,1536]{2,1,0:T(8,128)(2,1)S(1)}, bf16[2,1536,1536]{2,1,0:T(8,128)(2,1)}, u32[]{:S(2)}) copy-start(bf16[2,1536,1536]{2,1,0:T(8,128)(2,1)} %get-tuple-element.246) | copy-start | bytes 28311556 | tf_op jit(solution)/shard_map/while
  365.0 19.9 %collective-permute-start = (f32[2,1536,128]{1,2,0:T(8,128)S(1)}, f32[2,1536,128]{1,2,0:T(8,128)S(1)}, u32[]{:S(2)}, u32[]{:S(2)}) collective-permute-start(f32[2,1536,128]{1,2,0:T(8,128)S(1)} %maximum_add_fusion.3), channel_id=1, source_target_pairs={{3,0},{0,1},{1,2},{2,3},{7,4},{4,5},{5,6},{6,7},{11,8},{8,9},{9,10... | collective-permute-start | bytes 4718600 | tf_op jit(solution)/shard_map/while/body/eval_jaxpr/ppermute | solution.py:15
  384.9 8.5 %copy-start = (bf16[2,1536,1536]{2,1,0:T(8,128)(2,1)S(1)}, bf16[2,1536,1536]{2,1,0:T(8,128)(2,1)}, u32[]{:S(2)}) copy-start(bf16[2,1536,1536]{2,1,0:T(8,128)(2,1)} %get-tuple-element.246) | copy-start | bytes 28311556 | tf_op jit(solution)/shard_map/while
  398.9 19.9 %collective-permute-start = (f32[2,1536,128]{1,2,0:T(8,128)S(1)}, f32[2,1536,128]{1,2,0:T(8,128)S(1)}, u32[]{:S(2)}, u32[]{:S(2)}) collective-permute-start(f32[2,1536,128]{1,2,0:T(8,128)S(1)} %maximum_add_fusion.3), channel_id=1, source_target_pairs={{3,0},{0,1},{1,2},{2,3},{7,4},{4,5},{5,6},{6,7},{11,8},{8,9},{9,10... | collective-permute-start | bytes 4718600 | tf_op jit(solution)/shard_map/while/body/eval_jaxpr/ppermute | solution.py:15
  419.2 10.6 %slice-start = ((s8[9437184]{0:T(1024)(128)(4,1)}), s8[4194304]{0:T(1024)(128)(4,1)S(1)}, s32[]{:S(2)}) async-start(s8[9437184]{0:T(1024)(128)(4,1)} %bitcast.106), calls=%async_computation.1 | async-start | bytes 8388608
  419.3 10.6 %slice-start.1 = ((s8[9437184]{0:T(1024)(128)(4,1)}), s8[4194304]{0:T(1024)(128)(4,1)S(1)}, s32[]{:S(2)}) async-start(s8[9437184]{0:T(1024)(128)(4,1)} %bitcast.106), calls=%async_computation.2 | async-start | bytes 8388608
  424.5 5.3 %slice-start.2 = ((s8[9437184]{0:T(1024)(128)(4,1)}), s8[1048576]{0:T(1024)(128)(4,1)S(1)}, s32[]{:S(2)}) async-start(s8[9437184]{0:T(1024)(128)(4,1)} %bitcast.106), calls=%async_computation.3 | async-start | bytes 2097152
  434.7 1.4 copy-start.1
Sparse Core Ops, SparseCore 0:
  254.1 61.8 all-gather.1
where the time goes:
time: 449 us; the launch traced here: 446 us
  waiting for transfers between devices  227 us (51%)
  local copies, waits for them, and re-layouts  74.4 us (17%)
  other arithmetic  58 us (13%)
  matrix products  56.7 us (13%)
  starting transfers between devices  15.6 us (3%)
  between operations  13.6 us (3%)
    ppermute x11, waiting for transfers between devices, from_behind(): return lax.ppermute(block, axis, route)  185 us
    dot_general x16, matrix products, matmul(): return jnp.dot(first, second, preferred_element_type=jnp.float32)  56.7 us
    select_n x1, other arithmetic, local(): direct = jnp.where(dead_row[None, :, None], zero_bf, direct)  42 us
    all_gather x1, waiting for transfers between devices, local(): gathered = lax.all_gather(swapped, 'row', axis=2, tiled=True)  41.9 us
    unnamed x11, local copies, waits for them, and re-layouts  25.3 us
    scatter x2, local copies, waits for them, and re-layouts, local(): filled = direct.at[:, miss_row, :].set(patched)  20.5 us
    slice x1, local copies, waits for them, and re-layouts, complex_product(): left_tile[0]  19.5 us
    ppermute x11, starting transfers between devices, from_behind(): return lax.ppermute(block, axis, route)  15.6 us
  transfers between devices with their start and end apart: 12, of which 11 were waited for; matrix products, arithmetic and copies ran while one was open for 14% of the time, Pallas kernels for 0%

commit v1 on v0

v1 whole, which is shorter than its diff:
```python
import math

import jax
import jax.numpy as jnp
from jax import lax
from jax.sharding import PartitionSpec as P

F32 = jnp.float32
BF16 = jnp.bfloat16


def dot(first, second, dims=((1,), (0,)), **kw):
    return lax.dot_general(first, second, (dims, ((), ())), preferred_element_type=F32, **kw)


def make_local(order):
    def local(traces, recv_live, missing, wavelet):
        tile = traces.shape[1]
        grid = lax.axis_size("row")
        win = 128
        row = lax.axis_index("row")
        col = lax.axis_index("col")
        positions = jnp.arange(tile, dtype=jnp.int32)
        raw = traces[:, :, :win]
        gathered = lax.all_gather(raw, "row", axis=0, tiled=False)

        miss_row = lax.dynamic_index_in_dim(missing, row, 0, keepdims=False)
        miss_col = lax.dynamic_index_in_dim(missing, col, 0, keepdims=False)
        hot_row = positions[None, :] == miss_row[:, None]
        hot_col = positions[None, :] == miss_col[:, None]
        dead_row = jnp.any(hot_row, axis=0)
        dead_col = jnp.any(hot_col, axis=0)
        dead_win = jnp.any(missing[:, :, None] == positions[None, None, :win], axis=1)
        recv = (recv_live == 1).reshape(grid, tile)
        recv_row = lax.dynamic_index_in_dim(recv, row, 0, keepdims=False)
        recv_col = lax.dynamic_index_in_dim(recv, col, 0, keepdims=False)
        recv_miss_row = jnp.any(hot_row & recv_row[None, :], axis=1)
        recv_miss_col = jnp.any(hot_col & recv_col[None, :], axis=1)
        hot_row_b = hot_row.astype(BF16)
        hot_col_b = hot_col.astype(BF16)
        zero = jnp.zeros((), BF16)

        outgoing = jnp.stack([dot(hot_col_b, traces[p], ((1,), (1,))) for p in range(2)]).astype(BF16)
        route = [(r * grid + c, c * grid + r) for r in range(grid) for c in range(grid)]
        incoming = lax.ppermute(outgoing, ("row", "col"), route)
        dead_gather = lax.all_gather(outgoing[:, :, :win], "row", axis=0, tiled=False)

        swapped = lax.all_to_all(gathered, "col", split_axis=0, concat_axis=0, tiled=True)
        wide = jnp.transpose(swapped, (1, 2, 0, 3)).reshape(2, tile, grid * win)
        live_win = recv[:, :win].reshape(-1)
        keep = jnp.where(live_win[None, :] & ~dead_col[:, None], True, False)
        deads = jnp.transpose(dead_gather, (1, 2, 0, 3)).reshape(2, -1, grid * win)
        dead_keep = recv_miss_col[:, None] & ~dead_win.reshape(-1)[None, :]
        deads = jnp.where(dead_keep[None], deads, zero)
        window = [
            jnp.where(keep, wide[p], dot(hot_col_b, deads[p], ((0,), (0,))).astype(BF16))
            for p in range(2)
        ]
        masked = [jnp.where(recv_col[:, None], w, zero) for w in window]
        patched = jnp.where(recv_miss_row[None, :, None] & ~dead_col[None, None, :], incoming, zero)

        def product(left, right):
            first = jnp.concatenate([right[0], right[1]], axis=1)
            second = jnp.concatenate([-right[1], right[0]], axis=1)
            return dot(left[0], first) + dot(left[1], second)

        live = product(traces, masked)
        lost = product(patched, window)
        lost = dot(hot_row.astype(F32), lost, ((0,), (0,)), precision=lax.Precision.HIGHEST)
        partial = jnp.where(dead_row[:, None], lost, live)
        partial = jnp.transpose(partial.reshape(tile, 2, grid, win), (2, 1, 0, 3))
        total = lax.psum_scatter(partial, "col", scatter_dimension=0, tiled=True)[0]
        scale = 1.0 / math.sqrt(order)
        real = (wavelet[0] * total[0] - wavelet[1] * total[1]) * scale
        imag = (wavelet[0] * total[1] + wavelet[1] * total[0]) * scale
        own_in = lax.dynamic_index_in_dim(recv[:, :win], col, 0, keepdims=False)
        own_dead = jnp.where(
            recv_miss_row[None, :, None] & ~dead_col[None, None, :win], incoming[:, :, :win], zero
        )
        own = [
            jnp.where(
                dead_row[:, None],
                dot(hot_row_b, own_dead[p], ((0,), (0,))),
                jnp.where(own_in[None, :], raw[p], zero).astype(F32),
            )
            for p in range(2)
        ]
        return jnp.stack([own[0] - real, own[1] - imag])

    return local


def solution(mesh):
    in_specs = (P("freq", "row", "col"), P("freq"), P("freq", None), P("freq"))
    out_specs = P("freq", "row", "col")

    def run(traces, recv_live, missing, wavelet):
        local = make_local(traces.shape[1])
        return jax.shard_map(
            local, mesh=mesh, in_specs=in_specs, out_specs=out_specs, check_vma=False
        )(traces, recv_live, missing, wavelet)

    return run
```

time: 449 us -> 246 us (0.55)
  waiting for transfers between devices: 227 us -> 148 us
  local copies, waits for them, and re-layouts: 74.4 us -> 17 us
  other arithmetic: 58 us -> 9.83 us
  matrix products: 56.7 us -> 35.9 us
  blocking collectives: 0 us -> 10.9 us
  starting transfers between devices: 15.6 us -> 9.08 us
    ppermute x11 -> x1, waiting for transfers between devices: 185 us -> 0.01 us  [local(): incoming = lax.ppermute(outgoing, ('row', 'col'), route)]
    reduce_scatter x0 -> x1, waiting for transfers between devices: none -> 53.6 us  [local(): total = lax.psum_scatter(partial, 'col', scatter_dimension=0, tiled=True)[0]]
    select_n x7 -> x3, other arithmetic: 51.1 us -> 2.77 us  [the longest x1 1.95 us: local(): jnp.where(recv_miss_row[None, :, None] & ~dead_col[None, None, :], incomi...]
    all_gather x1, waiting for transfers between devices: 41.9 us -> 75.5 us  [local(): gathered = lax.all_gather(raw, 'row', axis=0, tiled=False)]
    unnamed x11 -> x28, local copies, waits for them, and re-layouts: 25.3 us -> 1.79 us
    dot_general x16 -> x11, matrix products: 56.7 us -> 35.9 us  [dot(): lax.dot_general(first, second, (dims, ((), ())), preferred_element_type=F...]
    scatter x2 -> x0, local copies, waits for them, and re-layouts: 20.5 us -> none  [local(): filled = direct.at[:, miss_row, :].set(patched)]
    all_to_all x0 -> x1, waiting for transfers between devices: none -> 18.6 us  [local(): lax.all_to_all(gathered, 'col', split_axis=0, concat_axis=0, tiled=True)]
  transfers between devices with their start and end apart: 12 -> 4, of which waited for: 11 -> 3; matrix products, arithmetic and copies ran while one was open for 14% -> 9% of each run, Pallas kernels for 0% -> 0%
where the time goes in v1:
time: 246 us; the launch traced here: 244 us
  waiting for transfers between devices  148 us (60%)
  matrix products  35.9 us (15%)
  local copies, waits for them, and re-layouts  17 us (7%)
  between operations  13.7 us (6%)
  blocking collectives  10.9 us (4%)
  other arithmetic  9.83 us (4%)
  starting transfers between devices  9.08 us (4%)
    all_gather x1, waiting for transfers between devices, local(): gathered = lax.all_gather(raw, 'row', axis=0, tiled=False)  75.5 us
    reduce_scatter x1, waiting for transfers between devices, local(): total = lax.psum_scatter(partial, 'col', scatter_dimension=0, tiled=True)[0]  53.6 us
    dot_general x11, matrix products, dot(): lax.dot_general(first, second, (dims, ((), ())), preferred_element_type=F...  35.9 us
    all_to_all x1, waiting for transfers between devices, local(): lax.all_to_all(gathered, 'col', split_axis=0, concat_axis=0, tiled=True)  18.6 us
    all_gather x1, blocking collectives, local(): lax.all_gather(outgoing[:, :, :win], 'row', axis=0, tiled=False)  10.9 us
    reshape x1, local copies, waits for them, and re-layouts, local(): partial = jnp.transpose(partial.reshape(tile, 2, grid, win), (2, 1, 0, 3))  6.58 us
  transfers between devices with their start and end apart: 4, of which 3 were waited for; matrix products, arithmetic and copies ran while one was open for 9% of the time, Pallas kernels for 0%

profile of v1, /device:TPU:1, one launch (start us, length us, event | category | flops | bytes accessed | tf_op | source)
XLA Modules:
  0.0 244.1 jit_solution(9473143310911814764)
XLA Ops:
  6.5 2.1 slice.88
  9.4 3.9 %fusion.36 = bf16[1,96,1536]{2,1,0:T(8,128)(2,1)S(1)} fusion(bf16[2,1536,1536]{2,1,0:T(8,128)(2,1)} %param.4, s32[96]{0:T(128)S(1)} %get-tuple-element.20), kind=kOutput, calls=%fused_computation.39 | convolution fusion | flops 453279744 | bytes 5013888 | tf_op jit(solution)/shard_map/dot_general | solution.py:13
  13.3 3.9 %fusion.39 = bf16[1,96,1536]{2,1,0:T(8,128)(2,1)S(1)} fusion(bf16[2,1536,1536]{2,1,0:T(8,128)(2,1)} %param.4, s32[96]{0:T(128)S(1)} %get-tuple-element.20), kind=kOutput, calls=%fused_computation.40 | convolution fusion | flops 453279744 | bytes 5013888 | tf_op jit(solution)/shard_map/dot_general | solution.py:13
  18.0 0.9 pad_maximum_fusion.1
  18.9 4.6 %collective-permute-start = (bf16[2,96,1536]{2,1,0:T(8,128)(2,1)}, bf16[2,96,1536]{2,1,0:T(8,128)(2,1)}, u32[]{:S(2)}, u32[]{:S(2)}) collective-permute-start(bf16[2,96,1536]{2,1,0:T(8,128)(2,1)} %pad_maximum_fusion.1), channel_id=1, source_target_pairs={{0,0},{1,4},{2,8},{3,12},{4,1},{5,5},{6,9},{7,13},{8,2},{9,6},{10,... | collective-permute-start | bytes 1769480 | tf_op jit(solution)/shard_map/ppermute | solution.py:45
  23.5 75.5 %all-gather.4.cloned.1.call-done = bf16[8,1536,128]{2,1,0:T(8,128)(2,1)} async-done(((bf16[2,1536,128]{2,1,0:T(8,128)(2,1)}), bf16[8,1536,128]{2,1,0:T(8,128)(2,1)}) %all-gather.4.cloned.1.call-update) | async-done | bytes 3145744 | tf_op jit(solution)/shard_map/all_gather | solution.py:25
  99.1 4.6 %copy.12 = bf16[4,2,1536,128]{2,3,1,0:T(8,128)(2,1)} copy(bf16[4,2,1536,128]{3,2,1,0:T(8,128)(2,1)} %bitcast.87) | data formatting | bytes 6291456 | tf_op jit(solution)/shard_map/all_gather | solution.py:25
  103.7 4.5 %all-to-all-start = ((bf16[4,2,1536,128]{2,3,1,0:T(8,128)(2,1)}), bf16[4,2,1536,128]{2,3,1,0:T(8,128)(2,1)S(1)}, u32[]{:S(2)}, u32[]{:S(2)}) async-start(bf16[4,2,1536,128]{2,3,1,0:T(8,128)(2,1)} %copy.12), calls=%async_computation | async-start | bytes 6291456 | tf_op jit(solution)/shard_map/all_to_all | solution.py:48
  108.2 1.0 fusion.48
  110.0 10.9 %all-gather.1 = bf16[8,96,128]{2,1,0:T(8,128)(2,1)S(1)} all-gather(bf16[2,96,128]{2,1,0:T(8,128)(2,1)S(1)} %fusion.58), channel_id=3, replica_groups=mesh['freq'=2,'row'=4,'col'=4] {'row'}, dimensions={0}, use_global_device_ids=true | all-gather | bytes 245760 | tf_op jit(solution)/shard_map/all_gather | solution.py:46
  122.8 0.8 broadcast_and_fusion
  123.6 1.9 broadcast_select_fusion.2
  125.6 18.6 %all-to-all-done = bf16[4,2,1536,128]{2,3,1,0:T(8,128)(2,1)S(1)} async-done(((bf16[4,2,1536,128]{2,3,1,0:T(8,128)(2,1)}), bf16[4,2,1536,128]{2,3,1,0:T(8,128)(2,1)S(1)}, u32[]{:S(2)}, u32[]{:S(2)}) %all-to-all-start) | async-done | bytes 3145760 | tf_op jit(solution)/shard_map/all_to_all | solution.py:48
  145.5 1.5 fusion.65
  147.0 7.1 %fusion = f32[1024,1536]{1,0:T(8,128)S(1)} fusion(bf16[2,1536,1536]{2,1,0:T(8,128)(2,1)} %param.4, bf16[1536,512]{0,1:T(8,128)(2,1)S(1)} %get-tuple-element.18, bf16[1536,512]{0,1:T(8,128)(2,1)S(1)} %get-tuple-element.11), kind=kOutput, calls=%fused_computation.1 | convolution fusion | flops 4838129664 | bytes 14155776 | tf_op jit(solution)/shard_map/dot_general | solution.py:13
  154.2 5.1 %fusion.4 = f32[1024,1536]{1,0:T(8,128)S(1)} fusion(bf16[2,1536,1536]{2,1,0:T(8,128)(2,1)S(1)} %bitcast.92, bf16[1536,512]{0,1:T(8,128)(2,1)S(1)} %get-tuple-element.12, bf16[1536,512]{0,1:T(8,128)(2,1)S(1)} %get-tuple-element.18), kind=kOutput, calls=%fused_computation.5 | convolution fusion | flops 4838129664 | bytes 14155776 | tf_op jit(solution)/shard_map/dot_general | solution.py:13
  159.2 1.1 fusion.16
  160.3 1.1 fusion.42
  161.4 5.0 %bitcast_select_fusion = f32[1536,1024]{0,1:T(8,128)} fusion(f32[1024,1536]{1,0:T(8,128)S(1)} %fusion.4, f32[1024,1536]{1,0:T(8,128)S(1)} %fusion, f32[96,1024]{1,0:T(8,128)S(1)} %fusion.42, pred[1536]{0:T(1024)(128)(4,1)S(1)} %copy-done.3, s32[96]{0:T(128)S(1)} %copy-done.6), kind=kOutput, calls=%fused_computation | convolution fusion | flops 1815232512 | bytes 19269504 | tf_op jit(solution)/shard_map/dot_general | solution.py:13
  166.4 6.6 %copy.14 = f32[1536,2,4,128]{3,0,1,2:T(8,128)} copy(f32[1536,2,4,128]{0,3,2,1:T(8,128)} %bitcast.84) | data formatting | bytes 12582912 | tf_op jit(solution)/shard_map/reshape | solution.py:71
  175.8 53.6 %reduce-scatter.2.cloned.1.call-done = f32[1,2,1536,128]{3,2,1,0:T(8,128)} async-done(((f32[4,2,1536,128]{3,2,1,0:T(8,128)}), f32[1,2,1536,128]{3,2,1,0:T(8,128)}) %reduce-scatter.2.cloned.1.call-update) | async-done | bytes 1572880 | tf_op jit(solution)/shard_map/reduce_scatter | solution.py:72
  229.4 3.3 %fusion.29 = f32[1,1536,128]{2,1,0:T(8,128)S(1)} fusion(f32[1,2,1536,128]{3,2,1,0:T(8,128)} %reduce-scatter.2.cloned.1.call-done, f32[]{:T(128)} %bitcast.25, f32[]{:T(128)} %bitcast.9, bf16[2,1536,1536]{2,1,0:T(8,128)(2,1)} %param.4, pred[1536]{0:T(1024)(128)(4,1)S(1)} %copy-done.3, pred[128]{0:T(512)(128)(4,1)S(1)} %dynamic-slice_bitcast_fusion, ...), kind=kOutput, calls=%fused_computation.36 | convolution fusion | flops 39469056 | bytes 2780168 | tf_op jit(solution)/shard_map/dot_general | solution.py:13
  232.7 3.3 %fusion.28 = f32[1,1536,128]{2,1,0:T(8,128)S(1)} fusion(f32[1,2,1536,128]{3,2,1,0:T(8,128)} %reduce-scatter.2.cloned.1.call-done, bf16[2,1536,1536]{2,1,0:T(8,128)(2,1)} %param.4, f32[]{:T(128)} %bitcast.25, f32[]{:T(128)} %bitcast.9, pred[1536]{0:T(1024)(128)(4,1)S(1)} %copy-done.3, pred[128]{0:T(512)(128)(4,1)S(1)} %dynamic-slice_bitcast_fusion, ...), kind=kOutput, calls=%fused_computation.35 | convolution fusion | flops 39469056 | bytes 2780168 | tf_op jit(solution)/shard_map/dot_general | solution.py:13
  236.0 1.2 pad_maximum_fusion
  (55 shorter events, 8.3 us)
Async XLA Ops:
  6.5 92.5 %all-gather.4.cloned.1.call-start = ((), (), s32[]{:S(2)}) async-start(), calls=%async_computation.3 | async-start | bytes 3932160 | tf_op jit(solution)/shard_map/all_gather | solution.py:25
  9.4 98.8 %copy-start.5 = (s32[96]{0:T(128)}, s32[96]{0:T(128)S(1)}, u32[]{:S(2)}) copy-start(s32[96]{0:T(128)S(1)} %get-tuple-element.19) | copy-start | bytes 1156
  9.4 98.8 %copy-start.7 = (s32[96]{0:T(128)}, s32[96]{0:T(128)S(1)}, u32[]{:S(2)}) copy-start(s32[96]{0:T(128)S(1)} %get-tuple-element.20) | copy-start | bytes 1156
  13.3 10.1 %copy-start.2 = (s32[6144]{0:T(1024)S(1)}, s32[6144]{0:T(1024)}, u32[]{:S(2)}) copy-start(s32[6144]{0:T(1024)} %param.5) | copy-start | bytes 73732
  17.3 0.7 copy-start
  18.9 104.8 %collective-permute-start = (bf16[2,96,1536]{2,1,0:T(8,128)(2,1)}, bf16[2,96,1536]{2,1,0:T(8,128)(2,1)}, u32[]{:S(2)}, u32[]{:S(2)}) collective-permute-start(bf16[2,96,1536]{2,1,0:T(8,128)(2,1)} %pad_maximum_fusion.1), channel_id=1, source_target_pairs={{0,0},{1,4},{2,8},{3,12},{4,1},{5,5},{6,9},{7,13},{8,2},{9,6},{10,... | collective-permute-start | bytes 1769480 | tf_op jit(solution)/shard_map/ppermute | solution.py:45
  103.7 40.4 %all-to-all-start = ((bf16[4,2,1536,128]{2,3,1,0:T(8,128)(2,1)}), bf16[4,2,1536,128]{2,3,1,0:T(8,128)(2,1)S(1)}, u32[]{:S(2)}, u32[]{:S(2)}) async-start(bf16[4,2,1536,128]{2,3,1,0:T(8,128)(2,1)} %copy.12), calls=%async_computation | async-start | bytes 6291456 | tf_op jit(solution)/shard_map/all_to_all | solution.py:48
  108.2 121.2 %reduce-scatter.2.cloned.1.call-start = ((), (), s32[]{:S(2)}) async-start(), calls=%async_computation.2 | async-start | bytes 7864320 | tf_op jit(solution)/shard_map/reduce_scatter | solution.py:72
  109.3 11.8 %copy-start.4 = (pred[1536]{0:T(1024)(128)(4,1)}, pred[1536]{0:T(1024)(128)(4,1)S(1)}, u32[]{:S(2)}) copy-start(pred[1536]{0:T(1024)(128)(4,1)S(1)} %get-tuple-element.24) | copy-start | bytes 4612
  144.2 0.6 copy-start.8
  145.5 8.7 %slice-start = ((s8[9437184]{0:T(1024)(128)(4,1)}), s8[4194304]{0:T(1024)(128)(4,1)S(1)}, s32[]{:S(2)}) async-start(s8[9437184]{0:T(1024)(128)(4,1)} %bitcast.91), calls=%async_computation.4 | async-start | bytes 8388608
  147.0 7.2 %slice-start.1 = ((s8[9437184]{0:T(1024)(128)(4,1)}), s8[4194304]{0:T(1024)(128)(4,1)S(1)}, s32[]{:S(2)}) async-start(s8[9437184]{0:T(1024)(128)(4,1)} %bitcast.91), calls=%async_computation.5 | async-start | bytes 8388608
  147.0 7.2 %slice-start.2 = ((s8[9437184]{0:T(1024)(128)(4,1)}), s8[1048576]{0:T(1024)(128)(4,1)S(1)}, s32[]{:S(2)}) async-start(s8[9437184]{0:T(1024)(128)(4,1)} %bitcast.91), calls=%async_computation.6 | async-start | bytes 2097152
  154.2 5.1 %copy-start.1 = (bf16[2,96,1536]{2,1,0:T(8,128)(2,1)S(1)}, bf16[2,96,1536]{2,1,0:T(8,128)(2,1)}, u32[]{:S(2)}) copy-start(bf16[2,96,1536]{2,1,0:T(8,128)(2,1)} %broadcast_select_fusion.2) | copy-start | bytes 1769476
  160.3 1.1 copy-start.3
  160.3 1.1 copy-start.6
  173.0 0.7 copy-start.10
  173.0 1.9 copy-start.9
Sparse Core Ops, SparseCore 0:
  8.9 90.1 all-gather.3
  173.1 56.1 reduce-scatter.1

commit v2 on v1

v2 whole, which is shorter than its diff:
```python
import functools
import math

import jax
import jax.numpy as jnp
from jax import lax
from jax.experimental import pallas as pl
from jax.experimental.pallas import tpu as pltpu
from jax.sharding import PartitionSpec as P

F32 = jnp.float32
BF16 = jnp.bfloat16
CHUNKS = 3
MESH = pl.DeviceIdType.MESH


def dot(first, second, dims=((1,), (0,))):
    return lax.dot_general(first, second, (dims, ((), ())), preferred_element_type=F32)


def kernel(
    grid, scale, wav, traces, hot_col, hot_col_t, hot_row_t, patch_keep, recv_lane, live_row,
    live_col, win_live, dead_keep, out,
    full, gath, wbuf, mir_out, mir_in, deads, wide, part_out, part_in,
    full_sem, own_sem, right_sem, left_sem, z_sem, across_sem, w_sem, mir_sem, dead_send, dead_recv,
    part_send, part_recv,
):
    row = lax.axis_index("row")
    col = lax.axis_index("col")
    tile = traces.shape[1]
    win = out.shape[2]
    chunk = tile // CHUNKS
    far = jnp.where(row > col, row - col, col - row)

    def remote(src, dst, send, recv, to_row, to_col):
        return pltpu.make_async_remote_copy(
            src_ref=src, dst_ref=dst, send_sem=send, recv_sem=recv,
            device_id={"row": to_row, "col": to_col}, device_id_type=MESH,
        )

    def right(c, p):
        return remote(gath.at[c, p], gath.at[c, p], right_sem.at[c, p], z_sem.at[c, p], row + 1, col)

    def left(c, p):
        return remote(gath.at[c, p], gath.at[c, p], left_sem.at[c, p], z_sem.at[c, p], row - 1, col)

    def across(c, b, p):
        return remote(gath.at[c, p], wbuf.at[b, p], across_sem.at[c, p], w_sem.at[b, p], row, c)

    def mirror():
        return remote(mir_out, mir_in, mir_sem.at[0], mir_sem.at[1], col, row)

    def dead(target, source):
        return remote(
            mir_out.at[:, :, pl.ds(0, win)], deads.at[source], dead_send.at[target],
            dead_recv.at[source], target, col,
        )

    def partial(b, source, k):
        span = pl.ds(k * chunk, chunk)
        return remote(
            part_out.at[b, :, span], part_in.at[source, :, span], part_send.at[b, k],
            part_recv.at[source, k], row, b,
        )

    owns = [
        pltpu.make_async_copy(traces.at[p, :, pl.ds(0, win)], gath.at[row, p], own_sem.at[p])
        for p in range(2)
    ]
    loads = [pltpu.make_async_copy(traces.at[p], full.at[p], full_sem.at[p]) for p in range(2)]
    for copy in owns + loads:
        copy.start()

    barrier = pltpu.get_barrier_semaphore()

    def greet(i, _):
        @pl.when(i != col)
        def _():
            pl.semaphore_signal(barrier, inc=1, device_id={"row": row, "col": i}, device_id_type=MESH)

        @pl.when(i != row)
        def _():
            pl.semaphore_signal(barrier, inc=1, device_id={"row": i, "col": col}, device_id_type=MESH)

        return 0

    lax.fori_loop(0, grid, greet, 0)

    @pl.when(row != col)
    def _():
        pl.semaphore_signal(barrier, inc=1, device_id={"row": col, "col": row}, device_id_type=MESH)
        pl.semaphore_wait(barrier, 2 * grid - 1)

    @pl.when(row == col)
    def _():
        pl.semaphore_wait(barrier, 2 * grid - 2)

    def pass_on(c, p, go_right, go_left):
        if go_right:
            @pl.when(row + 1 < grid)
            def _():
                right(c, p).start()

        if go_left:
            @pl.when(row > 0)
            def _():
                left(c, p).start()

        @pl.when(c != col)
        def _():
            across(c, col, p).start()

    for p in range(2):
        owns[p].wait()
        pass_on(row, p, True, True)

    for p in range(2):
        loads[p].wait()
        mir_out[p] = dot(hot_col[...], full[p], ((1,), (1,))).astype(BF16)

    @pl.when(row != col)
    def _():
        mirror().start()

    def send_dead(i, _):
        @pl.when(i != row)
        def _():
            dead(i, row).start()

        return 0

    lax.fori_loop(0, grid, send_dead, 0)

    def build_full():
        @pl.when(row != col)
        def _():
            mirror().wait_recv()
            mir_in[...] = mir_in[...] * patch_keep[...][None]

        @pl.when(row == col)
        def _():
            mir_in[...] = mir_out[...] * patch_keep[...][None]

        def some(k, _):
            span = pl.ds(pl.multiple_of(k * 128, 128), 128)
            for p in range(2):
                kept = full[p, span, :].astype(F32) * recv_lane[...] * live_row[span, :]
                full[p, span, :] = (kept + dot(hot_row_t[span, :], mir_in[p])).astype(BF16)
            return 0

        lax.fori_loop(0, tile // 128, some, 0)

    def widen(source, b, lost):
        for p in range(2):
            raw = source[p].astype(F32) * win_live[b] * live_col[...]
            extra = dot(hot_col_t[...], lost[p] * dead_keep[b])
            value = (raw + extra).astype(BF16)
            if p == 0:
                wide[0, :, :win] = value
                wide[1, :, win:] = value
            else:
                wide[0, :, win:] = value
                wide[1, :, :win] = -value

    def multiply():
        def block(t, _):
            chip = lax.rem(col // 2 + grid // 2 - 1 - t // 2, grid // 2)
            b = 2 * chip + lax.rem(col + 1 + t, 2)

            @pl.when(b != row)
            def _():
                dead(b, b).wait_recv()

            @pl.when(b == row)
            def _():
                deads[row] = mir_out[:, :, :win]

            @pl.when(b != col)
            def _():
                for p in range(2):
                    across(col, b, p).wait_recv()
                widen(wbuf.at[b], b, deads.at[b])

            @pl.when(b == col)
            def _():
                widen(gath.at[col], b, deads.at[b])

            def rows(k, _):
                span = pl.ds(pl.multiple_of(k * chunk, chunk), chunk)
                both = dot(full[0, span, :], wide[0]) + dot(full[1, span, :], wide[1])
                part_out[b, 0, span, :] = both[:, :win]
                part_out[b, 1, span, :] = both[:, win:]

                @pl.when(b != col)
                def _():
                    partial(b, col, k).start()

                return 0

            lax.fori_loop(0, CHUNKS, rows, 0)
            return 0

        lax.fori_loop(0, grid, block, 0)

    @pl.when(far == 0)
    def _():
        build_full()

    def step(s, _):
        @pl.when(s > 0)
        def _():
            for p in range(2):
                @pl.when(row - s >= 0)
                def _():
                    left(row - s, p).wait_recv()
                    pass_on(row - s, p, True, False)

                @pl.when(row + s < grid)
                def _():
                    right(row + s, p).wait_recv()
                    pass_on(row + s, p, False, True)

        @pl.when((s == 1) & (far > 0))
        def _():
            build_full()

        @pl.when(s == far)
        def _():
            multiply()

        return 0

    lax.fori_loop(0, grid, step, 0)

    def arrive(i, _):
        @pl.when(i != col)
        def _():
            for k in range(CHUNKS):
                partial(i, i, k).wait_recv()

        @pl.when(i == col)
        def _():
            part_in[col] = part_out[col]

        return 0

    lax.fori_loop(0, grid, arrive, 0)
    first, second = wav[0] * scale, wav[1] * scale

    def finish(k, _):
        span = pl.ds(pl.multiple_of(k * 128, 128), 128)
        real = part_in[0, 0, span, :]
        imag = part_in[0, 1, span, :]
        for i in range(1, grid):
            real = real + part_in[i, 0, span, :]
            imag = imag + part_in[i, 1, span, :]
        out[0, span, :] = full[0, span, :win].astype(F32) - (first * real - second * imag)
        out[1, span, :] = full[1, span, :win].astype(F32) - (first * imag + second * real)
        return 0

    lax.fori_loop(0, tile // 128, finish, 0)

    def drain(i, _):
        for p in range(2):
            @pl.when((row + 1 < grid) & (i <= row))
            def _():
                right(i, p).wait_send()

            @pl.when((row > 0) & (i >= row))
            def _():
                left(i, p).wait_send()

            @pl.when(i != col)
            def _():
                across(i, col, p).wait_send()

        @pl.when(i != row)
        def _():
            dead(i, row).wait_send()

        @pl.when(i != col)
        def _():
            for k in range(CHUNKS):
                partial(i, col, k).wait_send()

        return 0

    lax.fori_loop(0, grid, drain, 0)

    @pl.when(row != col)
    def _():
        mirror().wait_send()


def make_local(order):
    def local(traces, recv_live, missing, wavelet):
        tile = traces.shape[1]
        grid = lax.axis_size("row")
        lost = missing.shape[1]
        win = 128
        row = lax.axis_index("row")
        col = lax.axis_index("col")
        positions = jnp.arange(tile, dtype=jnp.int32)
        miss_row = lax.dynamic_index_in_dim(missing, row, 0, keepdims=False)
        miss_col = lax.dynamic_index_in_dim(missing, col, 0, keepdims=False)
        hot_row = positions[None, :] == miss_row[:, None]
        hot_col = positions[None, :] == miss_col[:, None]
        live_row = ~jnp.any(hot_row, axis=0)
        live_col = ~jnp.any(hot_col, axis=0)
        dead_win = jnp.any(missing[:, :, None] == positions[None, None, :win], axis=1)
        recv = (recv_live == 1).reshape(grid, tile)
        recv_row = lax.dynamic_index_in_dim(recv, row, 0, keepdims=False)
        recv_col = lax.dynamic_index_in_dim(recv, col, 0, keepdims=False)
        recv_miss_row = jnp.any(hot_row & recv_row[None, :], axis=1)
        recv_miss_col = jnp.any(hot_col & recv_col[None, :], axis=1)
        operands = (
            wavelet,
            traces,
            hot_col.astype(BF16),
            (positions[:, None] == miss_col[None, :]).astype(BF16),
            (positions[:, None] == miss_row[None, :]).astype(BF16),
            (recv_miss_row[:, None] & live_col[None, :]).astype(BF16),
            recv_col[None, :].astype(F32),
            live_row[:, None].astype(F32),
            live_col[:, None].astype(F32),
            recv[:, None, :win].astype(F32),
            (recv_miss_col[None, :, None] & ~dead_win[:, None, :]).astype(BF16),
        )
        vmem = pl.BlockSpec(memory_space=pltpu.VMEM)
        dma = pltpu.SemaphoreType.DMA
        return pl.pallas_call(
            functools.partial(kernel, grid, 1.0 / math.sqrt(order)),
            out_shape=jax.ShapeDtypeStruct((2, tile, win), F32),
            in_specs=[pl.BlockSpec(memory_space=pltpu.SMEM), pl.BlockSpec(memory_space=pl.ANY)]
            + [vmem] * 9,
            out_specs=vmem,
            scratch_shapes=[
                pltpu.VMEM((2, tile, tile), BF16),
                pltpu.VMEM((grid, 2, tile, win), BF16),
                pltpu.VMEM((grid, 2, tile, win), BF16),
                pltpu.VMEM((2, lost, tile), BF16),
                pltpu.VMEM((2, lost, tile), BF16),
                pltpu.VMEM((grid, 2, lost, win), BF16),
                pltpu.VMEM((2, tile, 2 * win), BF16),
                pltpu.VMEM((grid, 2, tile, win), F32),
                pltpu.VMEM((grid, 2, tile, win), F32),
                dma((2,)), dma((2,)), dma((grid, 2)), dma((grid, 2)), dma((grid, 2)),
                dma((grid, 2)), dma((grid, 2)), dma((2,)), dma((grid,)), dma((grid,)),
                dma((grid, CHUNKS)), dma((grid, CHUNKS)),
            ],
            compiler_params=pltpu.CompilerParams(
                collective_id=0, has_side_effects=True, vmem_limit_bytes=60 * 1024 * 1024
            ),
            name="predict",
        )(*operands)

    return local


def solution(mesh):
    in_specs = (P("freq", "row", "col"), P("freq"), P("freq", None), P("freq"))
    out_specs = P("freq", "row", "col")

    def run(traces, recv_live, missing, wavelet):
        local = make_local(traces.shape[1])
        return jax.shard_map(
            local, mesh=mesh, in_specs=in_specs, out_specs=out_specs, check_vma=False
        )(traces, recv_live, missing, wavelet)

    return run
```

time: 246 us -> 228 us (0.927)
  Pallas kernels: 0 us -> 215 us
  waiting for transfers between devices: 148 us -> 0 us
  matrix products: 35.9 us -> 0 us
  between operations: 13.7 us -> 0.04 us
  local copies, waits for them, and re-layouts: 17 us -> 5.74 us
  blocking collectives: 10.9 us -> 0 us
  starting transfers between devices: 9.08 us -> 0 us
  other arithmetic: 9.83 us -> 6.59 us
    pallas_call x0 -> x1, Pallas kernels: none -> 215 us  [local(): pl.pallas_call(functools.partial(kernel, grid, 1.0 / math.sqrt(order)), o...]
    all_gather x1 -> x0, waiting for transfers between devices: 75.5 us -> none  [local(): gathered = lax.all_gather(raw, 'row', axis=0, tiled=False)]
    reduce_scatter x1 -> x0, waiting for transfers between devices: 53.6 us -> none  [local(): total = lax.psum_scatter(partial, 'col', scatter_dimension=0, tiled=True)[0]]
    dot_general x11 -> x0, matrix products: 35.9 us -> none  [dot(): lax.dot_general(first, second, (dims, ((), ())), preferred_element_type=F...]
    all_to_all x1 -> x0, waiting for transfers between devices: 18.6 us -> none  [local(): lax.all_to_all(gathered, 'col', split_axis=0, concat_axis=0, tiled=True)]
    all_gather x1 -> x0, blocking collectives: 10.9 us -> none  [local(): lax.all_gather(outgoing[:, :, :win], 'row', axis=0, tiled=False)]
    reshape x2 -> x0, local copies, waits for them, and re-layouts: 6.67 us -> none  [the longest x1 6.58 us: local(): partial = jnp.transpose(partial.reshape(tile, 2, grid, win), (2, 1, 0, 3))]
    all_gather x2 -> x0, local copies, waits for them, and re-layouts: 4.79 us -> none  [the longest x1 4.64 us: local(): gathered = lax.all_gather(raw, 'row', axis=0, tiled=False)]
  transfers between devices with their start and end apart: 4 -> 0, of which waited for: 3 -> 0; matrix products, arithmetic and copies ran while one was open for 9% -> 0% of each run, Pallas kernels for 0% -> 0%
where the time goes in v2:
time: 228 us
  Pallas kernels  215 us (94%)
  other arithmetic  6.59 us (3%)
  local copies, waits for them, and re-layouts  5.74 us (3%)
    pallas_call x1, Pallas kernels, local(): pl.pallas_call(functools.partial(kernel, grid, 1.0 / math.sqrt(order)), o...  215 us

profile of v2, /device:TPU:1, one launch (start us, length us, event | category | flops | bytes accessed | tf_op | source)
XLA Modules:
  0.0 227.8 jit_solution(2898757455019214255)
XLA Ops:
  0.0 0.8 compare_reduce_fusion
  0.8 0.8 fusion.10
  1.6 0.7 broadcast_compare_fusion
  2.4 0.6 slice_convert_fusion
  3.0 0.6 dynamic-slice_reduce_fusion.1
  3.6 1.2 fusion.2
  4.8 0.7 and_convert_fusion.1.dead_keep
  5.5 0.8 and_convert_fusion.patch_keep
  6.3 1.2 reshape.53.live_col
  7.5 1.1 reshape.52.live_row
  8.6 1.1 fusion
  9.7 215.5 %predict.1 = f32[2,1536,128]{2,1,0:T(8,128)} custom-call(f32[2]{0:T(128)} %wav.1, bf16[2,1536,1536]{2,1,0:T(8,128)(2,1)} %traces.1, bf16[96,1536]{1,0:T(8,128)(2,1)} %get-tuple-element.19.hot_col, bf16[1536,96]{1,0:T(8,128)(2,1)} %get-tuple-element.17.hot_col_t, bf16[1536,96]{1,0:T(8,128)(2,1)} %get-tuple-element.18.hot_row_t, ...), custom_call_target="tpu_custom_call" | custom-call | tf_op jit(solution)/shard_map/predict/pallas_call | solution.py:331
  225.2 2.7 %copy.10 = f32[2,1536,128]{2,1,0:T(8,128)} copy(f32[2,1536,128]{2,1,0:T(8,128)} %predict.1) | data formatting | bytes 3145728
  (5 shorter events, 0.0 us)

commit v3 on v2

--- a/solution.py
+++ b/solution.py
@@ -21,16 +21,23 @@
 def kernel(
     grid, scale, wav, traces, hot_col, hot_col_t, hot_row_t, patch_keep, recv_lane, live_row,
     live_col, win_live, dead_keep, out,
-    full, gath, wbuf, mir_out, mir_in, deads, wide, part_out, part_in,
+    full, gath, wbuf, mir_out, mir_in, deads, wide, part_out, pair_in, chip_in,
     full_sem, own_sem, right_sem, left_sem, z_sem, across_sem, w_sem, mir_sem, dead_send, dead_recv,
-    part_send, part_recv,
+    pair_send, pair_recv, chip_send, chip_recv,
 ):
     row = lax.axis_index("row")
     col = lax.axis_index("col")
     tile = traces.shape[1]
     win = out.shape[2]
     chunk = tile // CHUNKS
+    chips = grid // 2
+    home = col // 2
+    side = lax.rem(col, 2)
+    mate = 2 * home + 1 - side
     far = jnp.where(row > col, row - col, col - row)
+    far_mate = jnp.where(row > mate, row - mate, mate - row)
+    turn = jnp.minimum(far + 1, grid - 1)
+    turn_mate = jnp.minimum(far_mate + 1, grid - 1)
 
     def remote(src, dst, send, recv, to_row, to_col):
         return pltpu.make_async_remote_copy(
@@ -56,12 +63,26 @@
             dead_recv.at[source], target, col,
         )
 
-    def partial(b, source, k):
+    def pair(chip, k):
         span = pl.ds(k * chunk, chunk)
         return remote(
-            part_out.at[b, :, span], part_in.at[source, :, span], part_send.at[b, k],
-            part_recv.at[source, k], row, b,
+            part_out.at[2 * chip + 1 - side, :, span], pair_in.at[chip, :, span],
+            pair_send.at[chip, k], pair_recv.at[chip, k], row, mate,
         )
+
+    def cross(chip, source, k):
+        span = pl.ds(k * chunk, chunk)
+        return remote(
+            part_out.at[2 * chip + side, :, span], chip_in.at[source, :, span],
+            chip_send.at[chip, k], chip_recv.at[source, k], row, 2 * chip + side,
+        )
+
+    def merge(chip, k):
+        pair(chip, k).wait_recv()
+        b = 2 * chip + side
+        span = pl.ds(pl.multiple_of(k * chunk, chunk), chunk)
+        part_out[b, :, span, :] = part_out[b, :, span, :] + pair_in[chip, :, span, :]
+        cross(chip, home, k).start()
 
     owns = [
         pltpu.make_async_copy(traces.at[p, :, pl.ds(0, win)], gath.at[row, p], own_sem.at[p])
@@ -164,7 +185,8 @@
 
     def multiply():
         def block(t, _):
-            chip = lax.rem(col // 2 + grid // 2 - 1 - t // 2, grid // 2)
+            chip = lax.rem(home + chips - 1 - t // 2, chips)
+            mine = lax.rem(t, 2)
             b = 2 * chip + lax.rem(col + 1 + t, 2)
 
             @pl.when(b != row)
@@ -191,9 +213,13 @@
                 part_out[b, 0, span, :] = both[:, :win]
                 part_out[b, 1, span, :] = both[:, win:]
 
-                @pl.when(b != col)
+                @pl.when(mine == 0)
                 def _():
-                    partial(b, col, k).start()
+                    pair(chip, k).start()
+
+                @pl.when((mine == 1) & (chip != home) & (far > far_mate))
+                def _():
+                    merge(chip, k)
 
                 return 0
 
@@ -220,40 +246,50 @@
                     right(row + s, p).wait_recv()
                     pass_on(row + s, p, False, True)
 
-        @pl.when((s == 1) & (far > 0))
+        @pl.when((s == min(2, grid - 1)) & (far > 0))
         def _():
             build_full()
 
-        @pl.when(s == far)
+        @pl.when(s == turn)
         def _():
             multiply()
 
+        @pl.when((s == turn_mate) & (far < far_mate))
+        def _():
+            def some(i, _):
+                for k in range(CHUNKS):
+                    merge(lax.rem(home + 1 + i, chips), k)
+                return 0
+
+            lax.fori_loop(0, chips - 1, some, 0)
+
         return 0
 
     lax.fori_loop(0, grid, step, 0)
 
     def arrive(i, _):
-        @pl.when(i != col)
-        def _():
-            for k in range(CHUNKS):
-                partial(i, i, k).wait_recv()
-
-        @pl.when(i == col)
-        def _():
-            part_in[col] = part_out[col]
-
-        return 0
-
-    lax.fori_loop(0, grid, arrive, 0)
+        for k in range(CHUNKS):
+            @pl.when(i != home)
+            def _():
+                cross(i, i, k).wait_recv()
+
+            @pl.when(i == home)
+            def _():
+                pair(home, k).wait_recv()
+
+        return 0
+
+    lax.fori_loop(0, chips, arrive, 0)
     first, second = wav[0] * scale, wav[1] * scale
 
     def finish(k, _):
         span = pl.ds(pl.multiple_of(k * 128, 128), 128)
-        real = part_in[0, 0, span, :]
-        imag = part_in[0, 1, span, :]
-        for i in range(1, grid):
-            real = real + part_in[i, 0, span, :]
-            imag = imag + part_in[i, 1, span, :]
+        real = part_out[col, 0, span, :] + pair_in[home, 0, span, :]
+        imag = part_out[col, 1, span, :] + pair_in[home, 1, span, :]
+        for i in range(1, chips):
+            other = lax.rem(home + i, chips)
+            real = real + chip_in[other, 0, span, :]
+            imag = imag + chip_in[other, 1, span, :]
         out[0, span, :] = full[0, span, :win].astype(F32) - (first * real - second * imag)
         out[1, span, :] = full[1, span, :win].astype(F32) - (first * imag + second * real)
         return 0
@@ -278,14 +314,21 @@
         def _():
             dead(i, row).wait_send()
 
-        @pl.when(i != col)
-        def _():
-            for k in range(CHUNKS):
-                partial(i, col, k).wait_send()
-
         return 0
 
     lax.fori_loop(0, grid, drain, 0)
+
+    def drain_sums(i, _):
+        for k in range(CHUNKS):
+            pair(i, k).wait_send()
+
+            @pl.when(i != home)
+            def _():
+                cross(i, home, k).wait_send()
+
+        return 0
+
+    lax.fori_loop(0, chips, drain_sums, 0)
 
     @pl.when(row != col)
     def _():
@@ -343,10 +386,12 @@
                 pltpu.VMEM((grid, 2, lost, win), BF16),
                 pltpu.VMEM((2, tile, 2 * win), BF16),
                 pltpu.VMEM((grid, 2, tile, win), F32),
-                pltpu.VMEM((grid, 2, tile, win), F32),
+                pltpu.VMEM((grid // 2, 2, tile, win), F32),
+                pltpu.VMEM((grid // 2, 2, tile, win), F32),
                 dma((2,)), dma((2,)), dma((grid, 2)), dma((grid, 2)), dma((grid, 2)),
                 dma((grid, 2)), dma((grid, 2)), dma((2,)), dma((grid,)), dma((grid,)),
-                dma((grid, CHUNKS)), dma((grid, CHUNKS)),
+                dma((grid // 2, CHUNKS)), dma((grid // 2, CHUNKS)),
+                dma((grid // 2, CHUNKS)), dma((grid // 2, CHUNKS)),
             ],
             compiler_params=pltpu.CompilerParams(
                 collective_id=0, has_side_effects=True, vmem_limit_bytes=60 * 1024 * 1024

time: 228 us -> 180 us (0.79)
  Pallas kernels: 215 us -> 168 us
    pallas_call x1, Pallas kernels: 215 us -> 168 us  [local(): pl.pallas_call(functools.partial(kernel, grid, 1.0 / math.sqrt(order)), o...]
where the time goes in v3:
time: 180 us
  Pallas kernels  168 us (93%)
  other arithmetic  6.59 us (4%)
  local copies, waits for them, and re-layouts  5.74 us (3%)
    pallas_call x1, Pallas kernels, local(): pl.pallas_call(functools.partial(kernel, grid, 1.0 / math.sqrt(order)), o...  168 us

profile of v3, /device:TPU:1, one launch (start us, length us, event | category | flops | bytes accessed | tf_op | source)
XLA Modules:
  0.0 179.9 jit_solution(15203451335656323390)
XLA Ops:
  0.0 0.8 compare_reduce_fusion
  0.8 0.8 fusion.10
  1.6 0.7 broadcast_compare_fusion
  2.4 0.6 slice_convert_fusion
  3.0 0.6 dynamic-slice_reduce_fusion.1
  3.6 1.2 fusion.2
  4.8 0.7 and_convert_fusion.1.dead_keep
  5.5 0.8 and_convert_fusion.patch_keep
  6.3 1.2 reshape.53.live_col
  7.5 1.1 reshape.52.live_row
  8.6 1.1 fusion
  9.7 167.6 %predict.1 = f32[2,1536,128]{2,1,0:T(8,128)} custom-call(f32[2]{0:T(128)} %wav.1, bf16[2,1536,1536]{2,1,0:T(8,128)(2,1)} %traces.1, bf16[96,1536]{1,0:T(8,128)(2,1)} %get-tuple-element.19.hot_col, bf16[1536,96]{1,0:T(8,128)(2,1)} %get-tuple-element.17.hot_col_t, bf16[1536,96]{1,0:T(8,128)(2,1)} %get-tuple-element.18.hot_row_t, ...), custom_call_target="tpu_custom_call" | custom-call | tf_op jit(solution)/shard_map/predict/pallas_call | solution.py:374
  177.3 2.7 %copy.10 = f32[2,1536,128]{2,1,0:T(8,128)} copy(f32[2,1536,128]{2,1,0:T(8,128)} %predict.1) | data formatting | bytes 3145728
  (5 shorter events, 0.0 us)

commit v4 on v3

--- a/solution.py
+++ b/solution.py
@@ -36,8 +36,9 @@
     mate = 2 * home + 1 - side
     far = jnp.where(row > col, row - col, col - row)
     far_mate = jnp.where(row > mate, row - mate, mate - row)
-    turn = jnp.minimum(far + 1, grid - 1)
-    turn_mate = jnp.minimum(far_mate + 1, grid - 1)
+    last = jnp.maximum(row, grid - 1 - row)
+    turn = jnp.minimum(far + 1, last)
+    inline = (far > far_mate) & (turn == last)
 
     def remote(src, dst, send, recv, to_row, to_col):
         return pltpu.make_async_remote_copy(
@@ -217,7 +218,7 @@
                 def _():
                     pair(chip, k).start()
 
-                @pl.when((mine == 1) & (chip != home) & (far > far_mate))
+                @pl.when((mine == 1) & (chip != home) & inline)
                 def _():
                     merge(chip, k)
 
@@ -254,7 +255,7 @@
         def _():
             multiply()
 
-        @pl.when((s == turn_mate) & (far < far_mate))
+        @pl.when((s == last) & jnp.logical_not(inline))
         def _():
             def some(i, _):
                 for k in range(CHUNKS):

time: 180 us -> 147 us (0.82)
  Pallas kernels: 168 us -> 135 us
    pallas_call x1, Pallas kernels: 168 us -> 135 us  [local(): pl.pallas_call(functools.partial(kernel, grid, 1.0 / math.sqrt(order)), o...]
where the time goes in v4:
time: 147 us
  Pallas kernels  135 us (92%)
  other arithmetic  6.59 us (4%)
  local copies, waits for them, and re-layouts  5.74 us (4%)
    pallas_call x1, Pallas kernels, local(): pl.pallas_call(functools.partial(kernel, grid, 1.0 / math.sqrt(order)), o...  135 us

profile of v4, /device:TPU:1, one launch (start us, length us, event | category | flops | bytes accessed | tf_op | source)
XLA Modules:
  0.0 146.9 jit_solution(968503168864377006)
XLA Ops:
  0.0 0.8 compare_reduce_fusion
  0.8 0.8 fusion.10
  1.6 0.7 broadcast_compare_fusion
  2.4 0.6 slice_convert_fusion
  3.0 0.6 dynamic-slice_reduce_fusion.1
  3.6 1.2 fusion.2
  4.8 0.7 and_convert_fusion.1.dead_keep
  5.5 0.8 and_convert_fusion.patch_keep
  6.3 1.2 reshape.53.live_col
  7.5 1.1 reshape.52.live_row
  8.6 1.1 fusion
  9.7 134.5 %predict.1 = f32[2,1536,128]{2,1,0:T(8,128)} custom-call(f32[2]{0:T(128)} %wav.1, bf16[2,1536,1536]{2,1,0:T(8,128)(2,1)} %traces.1, bf16[96,1536]{1,0:T(8,128)(2,1)} %get-tuple-element.19.hot_col, bf16[1536,96]{1,0:T(8,128)(2,1)} %get-tuple-element.17.hot_col_t, bf16[1536,96]{1,0:T(8,128)(2,1)} %get-tuple-element.18.hot_row_t, ...), custom_call_target="tpu_custom_call" | custom-call | tf_op jit(solution)/shard_map/predict/pallas_call | solution.py:375
  144.2 2.7 %copy.10 = f32[2,1536,128]{2,1,0:T(8,128)} copy(f32[2,1536,128]{2,1,0:T(8,128)} %predict.1) | data formatting | bytes 3145728
  (5 shorter events, 0.0 us)
